TPU v7x, 512 devices: a whole 4x4x16 slice. The times are simulated.
512 devices in a mesh: dp: 8 (over y_hi, x), feat: 64 (over y_lo, z, core).
Axes of the slice: x: 4, y: 4 (y_hi: 2, y_lo: 2; y = y_hi * 2 + y_lo), z: 16, core: 2. Of those that a mesh axis runs over, the one named last changes fastest.
Arguments:
- residuals: bfloat16 [384, 2, 8192], P('feat', None, 'dp'), may hold values from -6 to 6
- enc_w: bfloat16 [2, 8192, 16384], P(None, 'dp', 'feat'), may hold values from -0.046875 to 0.046875
- enc_b: float32 [16384], P('feat'), may hold values from 0.5 to 3
- dec_w: bfloat16 [2, 16384, 8192], P(None, 'feat', 'dp'), may hold values from -0.75 to 0.75
- dec_b: float32 [2, 8192], P(None, 'dp'), may hold values from -3 to 3
- active: int32 [384, 64], replicated, may hold values from 0 to 16383, all different within a row
Outputs:
- recon: bfloat16 [384, 2, 8192], P('feat', None, 'dp')
- enc_grad: bfloat16 [2, 8192, 16384], P(None, 'dp', 'feat')
- enc_bias_grad: float32 [16384], P('feat')
- dec_grad: bfloat16 [2, 16384, 8192], P(None, 'feat', 'dp')
- dec_bias_grad: float32 [2, 8192], P(None, 'dp')
Inputs may be any that keep to these rules, and one draw needn't show every extreme that they name: Each row of active names 64 different features, and every feature is named by some row.
All inputs are finite; a program needn't handle non-finite values.
Results may differ from a plain program's by a relative error of at most 0.0062.
Values may be sent and summed in bfloat16 or wider, within the bound.
A program may use at most 64 MiB of HBM per device.

v0:
```python
import math
import jax
import jax.numpy as jnp
from jax import lax
from jax.sharding import PartitionSpec as P


def feature_mask(active, first_feature, feat_dev):
    columns = first_feature + lax.iota(jnp.int32, feat_dev)
    total_rows, top_count = active.shape
    block_rows = math.gcd(total_rows, 64)
    grouped = active.reshape(total_rows // block_rows, block_rows, top_count)

    def one_block(row_group):
        return jnp.any(row_group[:, :, None] == columns[None, None, :], axis=1).astype(jnp.float32)

    return lax.map(one_block, grouped).reshape(total_rows, feat_dev)


def on_device(residuals, enc_w, enc_b, dec_w, dec_b, active):
    n_layers, width_dev, feat_dev = enc_w.shape
    gathered = lax.all_gather(residuals, "feat", axis=0, tiled=True)
    total_rows = gathered.shape[0]
    flat_in = gathered.reshape(total_rows, n_layers * width_dev)
    partial_value = jnp.dot(
        flat_in, enc_w.reshape(n_layers * width_dev, feat_dev), preferred_element_type=jnp.float32
    )
    pre_act = lax.psum(partial_value, "dp") + enc_b
    first_feature = lax.axis_index("feat") * feat_dev
    mask_table = feature_mask(active, first_feature, feat_dev)
    activation = (jnp.maximum(pre_act, 0.0) * mask_table).astype(jnp.bfloat16)
    rows_act = activation
    summed = lax.psum_scatter(
        jnp.einsum("tf,lfd->tld", rows_act, dec_w, preferred_element_type=jnp.float32),
        "feat",
        scatter_dimension=0,
        tiled=True,
    )
    recon_full = summed + dec_b[None]
    recon = recon_full.astype(jnp.bfloat16)
    resid_grad = ((recon_full - residuals.astype(jnp.float32)) * 0.25).astype(jnp.bfloat16)
    dec_bias_grad = lax.psum(jnp.sum(resid_grad.astype(jnp.float32), axis=0), "feat")
    shard_rows = lax.all_gather(resid_grad, "feat", axis=0, tiled=True)
    rows_act = activation
    dec_part = jnp.einsum("tf,tld->lfd", rows_act, shard_rows, preferred_element_type=jnp.float32)
    rows_grad = jnp.einsum("tld,lfd->tf", shard_rows, dec_w, preferred_element_type=jnp.float32)
    act_grad = lax.psum(rows_grad, "dp")
    pre_grad = jnp.where(activation > 0, act_grad, 0.0).astype(jnp.bfloat16)
    enc_bias_grad = jnp.sum(pre_grad.astype(jnp.float32), axis=0)
    enc_full = lax.dot_general(
        flat_in, pre_grad, (((0,), (0,)), ((), ())), preferred_element_type=jnp.float32
    )
    enc_grad = enc_full.reshape(n_layers, width_dev, feat_dev).astype(jnp.bfloat16)
    return (recon, enc_grad, enc_bias_grad, dec_part.astype(jnp.bfloat16), dec_bias_grad)


def solution(mesh):
    return jax.shard_map(
        on_device,
        mesh=mesh,
        in_specs=(
            P("feat", None, "dp"),
            P(None, "dp", "feat"),
            P("feat"),
            P(None, "feat", "dp"),
            P(None, "dp"),
            P(),
        ),
        out_specs=(
            P("feat", None, "dp"),
            P(None, "dp", "feat"),
            P("feat"),
            P(None, "feat", "dp"),
            P(None, "dp"),
        ),
        check_vma=False,
    )
```

profile of v0, /device:TPU:32, one launch (start us, length us, event | category | flops | bytes accessed | tf_op | source)
XLA Modules:
  0.0 868.6 jit_solution(2838763191016575245)
XLA Ops:
  7.2 0.0 copy-start
  7.2 0.0 all-gather.3.cloned.1.call-start
  7.2 0.7 all-gather.3.cloned.1.call-update
  7.9 0.0 all-reduce.5.cloned.1.call-start
  8.0 1.0 copy.33
  9.0 127.1 %all-gather.3.cloned.1.call-done = bf16[384,2,1024]{2,1,0:T(2,128)(2,1)} async-done(((bf16[6,2,1024]{2,1,0:T(2,128)(2,1)}), bf16[384,2,1024]{2,1,0:T(2,128)(2,1)}) %all-gather.3.cloned.1.call-update) | async-done | bytes 1572880 | tf_op jit(solution)/shard_map/all_gather | solution.py:22
  136.1 3.7 copy.36
  139.9 0.0 copy-start.3
  139.9 2.6 convolution_bitcast_fusion
  142.5 0.0 all-reduce.5.cloned.1.call-update
  142.5 0.0 all-reduce.7.cloned.1.call-start
  142.5 4.8 while.11
  142.6 0.7 compare_reduce_fusion.2
  143.4 0.7 compare_reduce_fusion.2
  144.2 0.7 compare_reduce_fusion.2
  144.9 0.7 compare_reduce_fusion.2
  145.7 0.7 compare_reduce_fusion.2
  146.5 0.7 compare_reduce_fusion.2
  147.3 92.5 %all-reduce.5.cloned.1.call-done = f32[384,256]{1,0:T(8,128)} async-done(((f32[384,256]{1,0:T(8,128)}), f32[384,256]{1,0:T(8,128)}) %all-reduce.5.cloned.1.call-update) | async-done | bytes 393232 | tf_op jit(solution)/shard_map/psum | solution.py:28
  239.8 0.0 copy-done.3
  239.8 1.1 fusion.12
  240.8 0.0 copy-done
  240.9 0.6 fusion.14
  241.4 4.1 copy.34
  245.6 0.0 copy-start.1
  245.6 0.0 copy-start.2
  245.6 0.0 all-reduce.7.cloned.1.call-update
  245.6 0.0 all-gather.5.cloned.1.call-start
  245.7 1.3 dynamic-slice
  247.6 439.7 %all-reduce.7.cloned.1.call-done = f32[384,2,1024]{2,1,0:T(2,128)} async-done(((f32[384,2,1024]{2,1,0:T(2,128)}), f32[384,2,1024]{2,1,0:T(2,128)}) %all-reduce.7.cloned.1.call-update) | async-done | bytes 3145744
  687.3 0.0 copy-done.1
  687.3 0.0 copy-done.2
  687.3 1.5 convert_reduce_fusion.1
  688.8 0.0 all-gather.5.cloned.1.call-update
  688.8 108.1 %psum.23 = f32[2,1024]{1,0:T(2,128)} all-reduce(f32[2,1024]{1,0:T(2,128)S(1)} %get-tuple-element.67), channel_id=1, replica_groups=mesh['dp'=8,'feat'=64] {'feat'}, use_global_device_ids=true, to_apply=%region_8.9 | all-reduce | flops 2048 | bytes 16384 | tf_op jit(solution)/shard_map/psum | solution.py:42
  796.9 9.1 %all-gather.5.cloned.1.call-done = bf16[384,2,1024]{2,1,0:T(2,128)(2,1)} async-done(((bf16[6,2,1024]{2,1,0:T(2,128)(2,1)}), bf16[384,2,1024]{2,1,0:T(2,128)(2,1)}) %all-gather.5.cloned.1.call-update) | async-done | bytes 1572880 | tf_op jit(solution)/shard_map/all_gather | solution.py:43
  806.0 2.0 fusion.9
  808.0 45.9 %all-reduce.8 = bf16[384,256]{1,0:T(8,128)(2,1)S(1)} all-reduce(f32[384,256]{1,0:T(8,128)S(1)} %fusion.9), channel_id=1, replica_groups=mesh['dp'=8,'feat'=64] {'dp'}, use_global_device_ids=true, to_apply=%region_5.6 | all-reduce | flops 98304 | bytes 589824 | tf_op jit(solution)/shard_map/psum | solution.py:47
  854.0 0.7 convert_reduce_fusion
  854.6 1.7 fusion.2
  856.3 2.3 copy.40
  858.6 2.2 fusion.6
  860.8 1.3 copy.39
  (19 shorter events, 0.1 us)
Async XLA Ops:
  7.2 233.7 %copy-start = (bf16[2,256,1024]{2,1,0:T(8,128)(2,1)S(1)}, bf16[2,256,1024]{2,1,0:T(8,128)(2,1)}, u32[]{:S(2)}) copy-start(bf16[2,256,1024]{2,1,0:T(8,128)(2,1)} %param.11) | copy-start | bytes 3145732
  7.2 128.9 %all-gather.3.cloned.1.call-start = ((), (), s32[]{:S(2)}) async-start(), calls=%async_computation | async-start | bytes 1597440 | tf_op jit(solution)/shard_map/all_gather | solution.py:22
  7.9 231.9 %all-reduce.5.cloned.1.call-start = ((), (), s32[]{:S(2)}) async-start(), calls=%async_computation.1 | async-start | bytes 786432 | tf_op jit(solution)/shard_map/psum | solution.py:28
  139.9 99.9 %copy-start.3 = (f32[256]{0:T(256)S(1)}, f32[256]{0:T(256)}, u32[]{:S(2)}) copy-start(f32[256]{0:T(256)} %param.10) | copy-start | bytes 3076
  142.5 544.8 %all-reduce.7.cloned.1.call-start = ((), (), s32[]{:S(2)}) async-start(), calls=%async_computation.3 | async-start | bytes 6291456
  245.6 441.7 %copy-start.1 = (bf16[6,2,1024]{2,1,0:T(2,128)(2,1)S(1)}, bf16[6,2,1024]{2,1,0:T(2,128)(2,1)}, u32[]{:S(2)}) copy-start(bf16[6,2,1024]{2,1,0:T(2,128)(2,1)} %param.8) | copy-start | bytes 73732
  245.6 441.7 %copy-start.2 = (f32[2,1024]{1,0:T(2,128)S(1)}, f32[2,1024]{1,0:T(2,128)}, u32[]{:S(2)}) copy-start(f32[2,1024]{1,0:T(2,128)} %param.12) | copy-start | bytes 24580
  245.6 560.4 %all-gather.5.cloned.1.call-start = ((), (), s32[]{:S(2)}) async-start(), calls=%async_computation.2 | async-start | bytes 1597440 | tf_op jit(solution)/shard_map/all_gather | solution.py:43
Sparse Core Ops, SparseCore 0:
  10.1 125.9 all-gather.2
  142.6 97.1 all-reduce.4
  245.7 441.5 all-reduce.6
  689.9 116.0 all-gather.4
where the time goes:
time: 869 us
  waiting for transfers between devices  669 us (77%)
  blocking collectives  154 us (18%)
  between operations  14.5 us (2%)
  local copies, waits for them, and re-layouts  13.8 us (2%)
  matrix products  9.11 us (1%)
    unnamed x5, waiting for transfers between devices  440 us
    all_gather x1, waiting for transfers between devices, on_device(): gathered = lax.all_gather(residuals, 'feat', axis=0, tiled=True)  127 us
    psum x1, blocking collectives, on_device(): lax.psum(jnp.sum(resid_grad.astype(jnp.float32), axis=0), 'feat')  108 us
    psum x1, waiting for transfers between devices, on_device(): pre_act = lax.psum(partial_value, 'dp') + enc_b  92.5 us
    psum x1, blocking collectives, on_device(): act_grad = lax.psum(rows_grad, 'dp')  45.9 us
  transfers between devices with their start and end apart: 4, of which 4 were waited for; matrix products, arithmetic and copies ran while one was open for 1% of the time, Pallas kernels for 0%

commit v1 on v0

--- a/solution.py
+++ b/solution.py
@@ -19,7 +19,14 @@
 
 def on_device(residuals, enc_w, enc_b, dec_w, dec_b, active):
     n_layers, width_dev, feat_dev = enc_w.shape
-    gathered = lax.all_gather(residuals, "feat", axis=0, tiled=True)
+
+    def put_goods(local_block, lane_axis):
+        return jnp.concatenate(
+            lax.all_to_all(jnp.stack([local_block] * lax.axis_size(lane_axis)), lane_axis, 0, 0),
+            axis=0,
+        )
+
+    gathered = put_goods(residuals, "feat")
     total_rows = gathered.shape[0]
     flat_in = gathered.reshape(total_rows, n_layers * width_dev)
     partial_value = jnp.dot(

time: 869 us -> 832 us (0.957)
  waiting for transfers between devices: 669 us -> 615 us
  starting transfers between devices: 0.16 us -> 17 us
    all_gather x1 -> x0, waiting for transfers between devices: 127 us -> none  [on_device(): gathered = lax.all_gather(residuals, 'feat', axis=0, tiled=True)]
    all_to_all x0 -> x1, waiting for transfers between devices: none -> 73.9 us  [put_goods(): lax.all_to_all(jnp.stack([local_block] * lax.axis_size(lane_axis)), lane_...]
    all_to_all x0 -> x1, starting transfers between devices: none -> 16.9 us  [put_goods(): lax.all_to_all(jnp.stack([local_block] * lax.axis_size(lane_axis)), lane_...]
    unnamed x5 -> x4, waiting for transfers between devices: 440 us -> 440 us
where the time goes in v1:
time: 832 us
  waiting for transfers between devices  615 us (74%)
  blocking collectives  154 us (19%)
  starting transfers between devices  17 us (2%)
  local copies, waits for them, and re-layouts  15.1 us (2%)
  between operations  14.5 us (2%)
    unnamed x4, waiting for transfers between devices  440 us
    psum x1, blocking collectives, on_device(): lax.psum(jnp.sum(resid_grad.astype(jnp.float32), axis=0), 'feat')  108 us
    psum x1, waiting for transfers between devices, on_device(): pre_act = lax.psum(partial_value, 'dp') + enc_b  92.5 us
    all_to_all x1, waiting for transfers between devices, put_goods(): lax.all_to_all(jnp.stack([local_block] * lax.axis_size(lane_axis)), lane_...  73.9 us
    psum x1, blocking collectives, on_device(): act_grad = lax.psum(rows_grad, 'dp')  45.9 us
    all_to_all x1, starting transfers between devices, put_goods(): lax.all_to_all(jnp.stack([local_block] * lax.axis_size(lane_axis)), lane_...  16.9 us
  transfers between devices with their start and end apart: 4, of which 4 were waited for; matrix products, arithmetic and copies ran while one was open for 1% of the time, Pallas kernels for 0%

profile of v1, /device:TPU:32, one launch (start us, length us, event | category | flops | bytes accessed | tf_op | source)
XLA Modules:
  0.0 831.8 jit_solution(13902866873323948643)
XLA Ops:
  7.2 0.0 copy-start
  7.2 2.8 stack.2
  10.0 0.0 copy-start.2
  10.0 16.9 %all-to-all-start = ((bf16[64,6,2,1024]{3,2,1,0:T(2,128)(2,1)}), bf16[64,6,2,1024]{3,2,1,0:T(2,128)(2,1)S(1)}, u32[]{:S(2)}, u32[]{:S(2)}) async-start(bf16[64,6,2,1024]{3,2,1,0:T(2,128)(2,1)} %stack.2), calls=%async_computation | async-start | bytes 3145728 | tf_op jit(solution)/shard_map/all_to_all | solution.py:25
  26.9 0.0 all-reduce.5.cloned.1.call-start
  26.9 0.0 copy-done.2
  27.0 0.1 copy.22
  27.1 73.9 %all-to-all-done = bf16[64,6,2,1024]{3,2,1,0:T(2,128)(2,1)S(1)} async-done(((bf16[64,6,2,1024]{3,2,1,0:T(2,128)(2,1)}), bf16[64,6,2,1024]{3,2,1,0:T(2,128)(2,1)S(1)}, u32[]{:S(2)}, u32[]{:S(2)}) %all-to-all-start) | async-done | bytes 1572896 | tf_op jit(solution)/shard_map/all_to_all | solution.py:25
  101.0 0.0 copy-start.1
  101.0 1.2 copy-done.1
  102.2 0.0 copy-start.6
  102.2 1.9 copy.29
  104.1 0.0 copy-done.6
  104.1 0.0 copy-start.5
  104.1 1.3 fusion.17
  105.5 0.0 all-reduce.5.cloned.1.call-update
  105.5 0.0 all-reduce.7.cloned.1.call-start
  105.5 4.8 while.11
  105.6 0.7 compare_reduce_fusion.2
  106.4 0.7 compare_reduce_fusion.2
  107.2 0.7 compare_reduce_fusion.2
  107.9 0.7 compare_reduce_fusion.2
  108.7 0.7 compare_reduce_fusion.2
  109.5 0.7 compare_reduce_fusion.2
  110.3 92.5 %all-reduce.5.cloned.1.call-done = f32[384,256]{1,0:T(8,128)} async-done(((f32[384,256]{1,0:T(8,128)}), f32[384,256]{1,0:T(8,128)}) %all-reduce.5.cloned.1.call-update) | async-done | bytes 393232 | tf_op jit(solution)/shard_map/psum | solution.py:35
  202.8 0.0 copy-done.5
  202.8 1.1 fusion.12
  203.8 0.0 copy-done
  203.9 0.6 fusion.14
  204.4 4.1 copy.23
  208.6 0.0 copy-start.3
  208.6 0.0 all-reduce.7.cloned.1.call-update
  208.6 0.0 all-gather.2.cloned.1.call-start
  208.6 1.3 dynamic-slice
  210.6 439.7 %all-reduce.7.cloned.1.call-done = f32[384,2,1024]{2,1,0:T(2,128)} async-done(((f32[384,2,1024]{2,1,0:T(2,128)}), f32[384,2,1024]{2,1,0:T(2,128)}) %all-reduce.7.cloned.1.call-update) | async-done | bytes 3145744
  650.3 0.0 copy-done.3
  650.3 0.0 copy-done.4
  650.3 1.5 convert_reduce_fusion.1
  651.8 0.0 all-gather.2.cloned.1.call-update
  651.8 108.2 %psum.23 = f32[2,1024]{1,0:T(2,128)} all-reduce(f32[2,1024]{1,0:T(2,128)S(1)} %get-tuple-element.62), channel_id=1, replica_groups=mesh['dp'=8,'feat'=64] {'feat'}, use_global_device_ids=true, to_apply=%region_8.9 | all-reduce | flops 2048 | bytes 16384 | tf_op jit(solution)/shard_map/psum | solution.py:49
  760.0 9.2 %all-gather.2.cloned.1.call-done = bf16[384,2,1024]{2,1,0:T(2,128)(2,1)} async-done(((bf16[6,2,1024]{2,1,0:T(2,128)(2,1)}), bf16[384,2,1024]{2,1,0:T(2,128)(2,1)}) %all-gather.2.cloned.1.call-update) | async-done | bytes 1572880 | tf_op jit(solution)/shard_map/all_gather | solution.py:50
  769.2 2.0 fusion.9
  771.2 45.9 %all-reduce.8 = bf16[384,256]{1,0:T(8,128)(2,1)S(1)} all-reduce(f32[384,256]{1,0:T(8,128)S(1)} %fusion.9), channel_id=1, replica_groups=mesh['dp'=8,'feat'=64] {'dp'}, use_global_device_ids=true, to_apply=%region_5.6 | all-reduce | flops 98304 | bytes 589824 | tf_op jit(solution)/shard_map/psum | solution.py:54
  817.1 1.7 fusion.2
  818.8 0.7 convert_reduce_fusion
  819.5 2.3 copy.28
  821.7 2.2 fusion.6
  823.9 1.3 copy.27
  (20 shorter events, 0.1 us)
Async XLA Ops:
  7.2 196.7 %copy-start = (bf16[2,256,1024]{2,1,0:T(8,128)(2,1)S(1)}, bf16[2,256,1024]{2,1,0:T(8,128)(2,1)}, u32[]{:S(2)}) copy-start(bf16[2,256,1024]{2,1,0:T(8,128)(2,1)} %param.11) | copy-start | bytes 3145732
  10.0 17.0 %copy-start.2 = (s32[384,64]{0,1:T(8,128)S(1)}, s32[384,64]{0,1:T(8,128)}, u32[]{:S(2)}) copy-start(s32[384,64]{0,1:T(8,128)} %param.13) | copy-start | bytes 294916
  10.0 91.0 %all-to-all-start = ((bf16[64,6,2,1024]{3,2,1,0:T(2,128)(2,1)}), bf16[64,6,2,1024]{3,2,1,0:T(2,128)(2,1)S(1)}, u32[]{:S(2)}, u32[]{:S(2)}) async-start(bf16[64,6,2,1024]{3,2,1,0:T(2,128)(2,1)} %stack.2), calls=%async_computation | async-start | bytes 3145728 | tf_op jit(solution)/shard_map/all_to_all | solution.py:25
  26.9 175.9 %all-reduce.5.cloned.1.call-start = ((), (), s32[]{:S(2)}) async-start(), calls=%async_computation.1 | async-start | bytes 786432 | tf_op jit(solution)/shard_map/psum | solution.py:35
  101.0 1.2 copy-start.1
  102.2 1.9 copy-start.6
  104.1 98.7 %copy-start.5 = (f32[256]{0:T(256)S(1)}, f32[256]{0:T(256)}, u32[]{:S(2)}) copy-start(f32[256]{0:T(256)} %param.10) | copy-start | bytes 3076
  105.5 544.8 %all-reduce.7.cloned.1.call-start = ((), (), s32[]{:S(2)}) async-start(), calls=%async_computation.3 | async-start | bytes 6291456
  208.6 441.7 %copy-start.3 = (bf16[6,2,1024]{2,1,0:T(2,128)(2,1)S(1)}, bf16[6,2,1024]{2,1,0:T(2,128)(2,1)}, u32[]{:S(2)}) copy-start(bf16[6,2,1024]{2,1,0:T(2,128)(2,1)} %param.8) | copy-start | bytes 73732
  208.6 441.7 %copy-start.4 = (f32[2,1024]{1,0:T(2,128)S(1)}, f32[2,1024]{1,0:T(2,128)}, u32[]{:S(2)}) copy-start(f32[2,1024]{1,0:T(2,128)} %param.12) | copy-start | bytes 24580
  208.6 560.6 %all-gather.2.cloned.1.call-start = ((), (), s32[]{:S(2)}) async-start(), calls=%async_computation.2 | async-start | bytes 1597440 | tf_op jit(solution)/shard_map/all_gather | solution.py:50
Sparse Core Ops, SparseCore 0:
  105.6 97.1 all-reduce.4
  208.7 441.5 all-reduce.6
  653.0 116.1 all-gather.1
